TPU v7x, 32 devices: a whole 2x2x4 slice. The times are simulated.
32 devices in a mesh: rep: 4 (over y, core), seq: 2 (over x), ctx: 4 (over z).
Axes of the slice: x: 2, y: 2, z: 4, core: 2. Of those that a mesh axis runs over, the one named last changes fastest.
Arguments:
- tokens: bfloat16 [8192, 2048], P(('rep', 'seq', 'ctx')), may hold values from -6 to 6
- cotangent: bfloat16 [8192, 2048], P(('rep', 'seq', 'ctx')), may hold values from -6 to 6
- document_index: int32 [8192], P(('rep', 'seq')), may hold values from 0 to 10, as said below
- padding_token_mask: int32 [8192], P(('rep', 'seq')), may hold values from 0 to 1, as said below
- attention_gain: bfloat16 [2048], P(('seq', 'ctx')), may hold values from 0.099609375 to 1.8984375
- projection_weight: bfloat16 [2048, 6144], P(('seq', 'ctx')), may hold values from -0.125 to 0.125
- head_gain: bfloat16 [2, 128], replicated, may hold values from 0.099609375 to 1.8984375
- out_weight: bfloat16 [2048, 2048], P(('seq', 'ctx')), may hold values from -2 to 2
- feedforward_gain: bfloat16 [2048], P(('seq', 'ctx')), may hold values from 0.099609375 to 1.8984375
- gate_weight: bfloat16 [2048, 6144], P(('seq', 'ctx')), may hold values from -0.125 to 0.125
- up_weight: bfloat16 [2048, 6144], P(('seq', 'ctx')), may hold values from -0.125 to 0.125
- down_weight: bfloat16 [2048, 6144], P(('seq', 'ctx')), may hold values from -0.078125 to 0.078125
Outputs:
- layer_out: bfloat16 [8192, 2048], P(('rep', 'seq', 'ctx'))
- tokens_grad: bfloat16 [8192, 2048], P(('rep', 'seq', 'ctx'))
- attention_gain_grad: float32 [2048], P(('seq', 'ctx'))
- proj_weight_grad: float32 [2048, 6144], P(('seq', 'ctx'))
- head_gain_grad: float32 [2, 128], replicated
- out_weight_grad: float32 [2048, 2048], P(('seq', 'ctx'))
- feedforward_gain_grad: float32 [2048], P(('seq', 'ctx'))
- gate_weight_grad: float32 [2048, 6144], P(('seq', 'ctx'))
- up_weight_grad: float32 [2048, 6144], P(('seq', 'ctx'))
- down_weight_grad: float32 [2048, 6144], P(('seq', 'ctx'))
Inputs may be any that keep to these rules, and one draw needn't show every extreme that they name: `document_index`: along each sequence of 1024 tokens the ids never fall. `padding_token_mask`: the zeros of a sequence form one run at its end.
All inputs are finite; a program needn't handle non-finite values.
Results may differ from a plain program's by a relative error of at most 0.02.
Values may be sent and summed in bfloat16 or wider, within the bound.
A program may use at most 640 MiB of HBM per device.

v0:
```python
import jax
import jax.numpy as jnp
from jax import lax
from jax.sharding import PartitionSpec as P

QUERY_HEADS = 16
KEY_VALUE_HEADS = 8
HEAD_SIZE = 128
norm_epsilon = 1e-06
rope_base = 1000000.0
masked_value = -1e30
contract_rows = (((0,), (0,)), ((), ()))
contract_cols = (((1,), (1,)), ((), ()))


def rope_tables(positions):
    half_size = HEAD_SIZE // 2
    frequency = rope_base ** (-2.0 * jnp.arange(half_size, dtype=jnp.float32) / HEAD_SIZE)
    angles = positions.astype(jnp.float32)[:, None, None] * frequency[None, None, :]
    return (jnp.cos(angles), jnp.sin(angles))


def rotate(value_rows, cosine_table, sine_table):
    half_size = value_rows.shape[-1] // 2
    first_half = value_rows[..., :half_size]
    second_half = value_rows[..., half_size:]
    return jnp.concatenate(
        [
            first_half * cosine_table - second_half * sine_table,
            second_half * cosine_table + first_half * sine_table,
        ],
        axis=-1,
    )


def inverse_rotation(grads, cosine_table, sine_table):
    half_size = grads.shape[-1] // 2
    first_half = grads[..., :half_size]
    second_half = grads[..., half_size:]
    return jnp.concatenate(
        [
            first_half * cosine_table + second_half * sine_table,
            second_half * cosine_table - first_half * sine_table,
        ],
        axis=-1,
    )


def head_norm(value_rows, gain):
    root_factor = lax.rsqrt(
        jnp.mean(value_rows * value_rows, axis=-1, keepdims=True) + norm_epsilon
    )
    unit_values = value_rows * root_factor
    return (unit_values * gain, unit_values, root_factor)


def norm_back(grad_out, unit_values, root_factor, gain):
    scaled = grad_out * gain
    return root_factor * (
        scaled - unit_values * jnp.mean(scaled * unit_values, axis=-1, keepdims=True)
    )


def over_replicas(grad_parts):
    return (
        lax.psum(grad_parts[0].astype(jnp.bfloat16), "rep").astype(jnp.float32),
        lax.psum(grad_parts[1].astype(jnp.bfloat16), "rep").astype(jnp.float32),
    )


def per_device(
    tokens,
    cotangent,
    document_index,
    padding_token_mask,
    attention_gain,
    projection_weight,
    head_gain,
    out_weight,
    feedforward_gain,
    gate_weight,
    up_weight,
    down_weight,
):
    token_rows = tokens.shape[0]
    sequence_length = document_index.shape[0]
    shard_rows = projection_weight.shape[0]
    proj_width = projection_weight.shape[1]
    ff_width = gate_weight.shape[1]
    query_total_width = QUERY_HEADS * HEAD_SIZE
    key_total_width = KEY_VALUE_HEADS * HEAD_SIZE
    query_group_width = QUERY_HEADS // KEY_VALUE_HEADS
    score_scale = HEAD_SIZE ** (-0.5)
    tokens_wide = tokens.astype(jnp.float32)
    root_attn = lax.rsqrt(jnp.mean(tokens_wide * tokens_wide, axis=1, keepdims=True) + norm_epsilon)
    unit_attn = tokens_wide * root_attn
    gain_piece = lax.all_gather(attention_gain, ("seq", "ctx"), axis=0, tiled=True)
    weight_piece = lax.all_gather(projection_weight, ("seq", "ctx"), axis=0, tiled=True)
    columns = unit_attn
    normed = (columns * gain_piece.astype(jnp.float32)).astype(jnp.bfloat16)
    result = (
        jnp.dot(normed, weight_piece, preferred_element_type=jnp.float32),
        gain_piece.astype(jnp.float32),
        normed,
    )
    folded_proj = result
    projected_rows = folded_proj[0]
    gain_attn_full = folded_proj[1]
    normed_attn = folded_proj[2]
    queries_raw = projected_rows[:, :query_total_width].reshape(token_rows, QUERY_HEADS, HEAD_SIZE)
    gate_logits = projected_rows[:, query_total_width : 2 * query_total_width]
    keys_raw = projected_rows[
        :, 2 * query_total_width : 2 * query_total_width + key_total_width
    ].reshape(token_rows, KEY_VALUE_HEADS, HEAD_SIZE)
    values_raw = projected_rows[:, 2 * query_total_width + key_total_width :]
    first_row = lax.axis_index("ctx") * token_rows
    positions = first_row + jnp.arange(token_rows, dtype=jnp.int32)
    cosine_table, sine_table = rope_tables(positions)
    head_gain_wide = head_gain.astype(jnp.float32)
    query_normed, query_unit, query_root = head_norm(queries_raw, head_gain_wide[0])
    key_normed, key_unit, key_root = head_norm(keys_raw, head_gain_wide[1])
    query_low = (
        rotate(query_normed, cosine_table, sine_table)
        .astype(jnp.bfloat16)
        .reshape(token_rows, KEY_VALUE_HEADS, query_group_width, HEAD_SIZE)
    )
    key_low = (
        rotate(key_normed, cosine_table, sine_table)
        .astype(jnp.bfloat16)
        .reshape(token_rows, key_total_width)
    )
    value_low = values_raw.astype(jnp.bfloat16)
    every_key, every_value = (
        lax.all_gather(key_low, "ctx", axis=0, tiled=True),
        lax.all_gather(value_low, "ctx", axis=0, tiled=True),
    )
    every_key = every_key.reshape(sequence_length, KEY_VALUE_HEADS, HEAD_SIZE)
    every_value = every_value.reshape(sequence_length, KEY_VALUE_HEADS, HEAD_SIZE)
    seg_here = lax.dynamic_slice_in_dim(document_index, first_row, token_rows, 0)
    pad_here = lax.dynamic_slice_in_dim(padding_token_mask, first_row, token_rows, 0)
    key_places = jnp.arange(sequence_length, dtype=jnp.int32)
    allowed = (seg_here[:, None] == document_index[None, :]) & (
        key_places[None, :] <= positions[:, None]
    ) & (padding_token_mask[None, :] == 1) | (key_places[None, :] == positions[:, None])

    def masked_scores():
        raw_scores = (
            jnp.einsum("qhgd,khd->hgqk", query_low, every_key, preferred_element_type=jnp.float32)
            * score_scale
        )
        return jnp.where(allowed[None, None], raw_scores, masked_value)

    scores = masked_scores()
    peak = jnp.max(scores, axis=3, keepdims=True)
    exp_scores = jnp.exp(scores - peak)
    denominator = jnp.sum(exp_scores, axis=3, keepdims=True)
    log_total = peak + jnp.log(denominator)
    probs_low = (exp_scores / denominator).astype(jnp.bfloat16)
    attended_rows = jnp.einsum(
        "hgqk,khd->qhgd", probs_low, every_value, preferred_element_type=jnp.float32
    ).reshape(token_rows, query_total_width)
    gate_activations = jax.nn.sigmoid(gate_logits)
    mixed_heads = (attended_rows * gate_activations).astype(jnp.bfloat16)
    columns = lax.dot_general(
        mixed_heads,
        lax.all_gather(out_weight, ("seq", "ctx"), axis=0, tiled=True),
        contract_cols,
        preferred_element_type=jnp.float32,
    )
    result = (columns,)
    folded_out = result
    resid_mid = tokens_wide + folded_out[0]
    root_mlp = lax.rsqrt(jnp.mean(resid_mid * resid_mid, axis=1, keepdims=True) + norm_epsilon)
    unit_mlp = resid_mid * root_mlp
    gain_piece = lax.all_gather(feedforward_gain, ("seq", "ctx"), axis=0, tiled=True)
    gate_piece = lax.all_gather(gate_weight, ("seq", "ctx"), axis=0, tiled=True)
    up_piece = lax.all_gather(up_weight, ("seq", "ctx"), axis=0, tiled=True)
    columns = unit_mlp
    normed = (columns * gain_piece.astype(jnp.float32)).astype(jnp.bfloat16)
    result = (
        jnp.dot(normed, gate_piece, preferred_element_type=jnp.float32),
        jnp.dot(normed, up_piece, preferred_element_type=jnp.float32),
        gain_piece.astype(jnp.float32),
        normed,
    )
    folded_mlp = result
    gate_lin = folded_mlp[0]
    up_lin = folded_mlp[1]
    gain_mlp_full = folded_mlp[2]
    normed_mlp = folded_mlp[3]
    gate_sig = jax.nn.sigmoid(gate_lin)
    silu_gate = gate_lin * gate_sig
    hidden_low = (silu_gate * up_lin).astype(jnp.bfloat16)
    columns = lax.dot_general(
        hidden_low,
        lax.all_gather(down_weight, ("seq", "ctx"), axis=0, tiled=True),
        contract_cols,
        preferred_element_type=jnp.float32,
    )
    result = (columns,)
    layer_out = (resid_mid + result[0]).astype(jnp.bfloat16)
    masked_grad = cotangent.astype(jnp.float32) * pad_here.astype(jnp.float32)[:, None]
    d_out_low = masked_grad.astype(jnp.bfloat16)
    columns = d_out_low
    d_hidden = jnp.dot(
        columns,
        lax.all_gather(down_weight, ("seq", "ctx"), axis=0, tiled=True),
        preferred_element_type=jnp.float32,
    )
    d_gate_low = (d_hidden * up_lin * gate_sig * (1.0 + gate_lin * (1.0 - gate_sig))).astype(
        jnp.bfloat16
    )
    d_up_low = (d_hidden * silu_gate).astype(jnp.bfloat16)
    gate_piece = lax.all_gather(gate_weight, ("seq", "ctx"), axis=0, tiled=True)
    up_piece = lax.all_gather(up_weight, ("seq", "ctx"), axis=0, tiled=True)
    columns = lax.dot_general(
        d_gate_low, gate_piece, contract_cols, preferred_element_type=jnp.float32
    ) + lax.dot_general(d_up_low, up_piece, contract_cols, preferred_element_type=jnp.float32)
    d_normed_mlp = columns
    normed_rows = normed_mlp
    grad_rows = d_out_low
    mlp_grads = lax.psum_scatter(
        jnp.concatenate(
            [
                lax.dot_general(
                    normed_rows, d_gate_low, contract_rows, preferred_element_type=jnp.float32
                ),
                lax.dot_general(
                    normed_rows, d_up_low, contract_rows, preferred_element_type=jnp.float32
                ),
                lax.dot_general(
                    grad_rows, hidden_low, contract_rows, preferred_element_type=jnp.float32
                ),
            ],
            axis=1,
        ).astype(jnp.bfloat16),
        ("seq", "ctx"),
        scatter_dimension=0,
        tiled=True,
    ).astype(jnp.float32)
    gain_mlp_term = jnp.sum(d_normed_mlp * unit_mlp, axis=0)
    d_resid_mid = masked_grad + norm_back(d_normed_mlp, unit_mlp, root_mlp, gain_mlp_full)
    d_attn_low = d_resid_mid.astype(jnp.bfloat16)
    columns = d_attn_low
    mixed_gradient = jnp.dot(
        columns,
        lax.all_gather(out_weight, ("seq", "ctx"), axis=0, tiled=True),
        preferred_element_type=jnp.float32,
    )
    d_gate_logits = mixed_gradient * attended_rows * gate_activations * (1.0 - gate_activations)
    d_attended_low = (
        (mixed_gradient * gate_activations)
        .astype(jnp.bfloat16)
        .reshape(token_rows, KEY_VALUE_HEADS, query_group_width, HEAD_SIZE)
    )
    probs = jnp.exp(masked_scores() - log_total)
    d_probs = jnp.einsum(
        "qhgd,khd->hgqk", d_attended_low, every_value, preferred_element_type=jnp.float32
    )
    value_term = jnp.einsum(
        "hgqk,qhgd->khd", probs_low, d_attended_low, preferred_element_type=jnp.float32
    )
    delta = jnp.sum(probs * d_probs, axis=3, keepdims=True)
    d_scores_low = (probs * (d_probs - delta)).astype(jnp.bfloat16)
    d_queries = (
        jnp.einsum("hgqk,khd->qhgd", d_scores_low, every_key, preferred_element_type=jnp.float32)
        * score_scale
    )
    key_term = (
        jnp.einsum("hgqk,qhgd->khd", d_scores_low, query_low, preferred_element_type=jnp.float32)
        * score_scale
    )
    key_gradient, d_values = (
        lax.psum_scatter(
            key_term.reshape(sequence_length, key_total_width).astype(jnp.bfloat16),
            "ctx",
            scatter_dimension=0,
            tiled=True,
        ).astype(jnp.float32),
        lax.psum_scatter(
            value_term.reshape(sequence_length, key_total_width).astype(jnp.bfloat16),
            "ctx",
            scatter_dimension=0,
            tiled=True,
        ).astype(jnp.float32),
    )
    d_query_normed = inverse_rotation(
        d_queries.reshape(token_rows, QUERY_HEADS, HEAD_SIZE), cosine_table, sine_table
    )
    normed_key_gradient = inverse_rotation(
        key_gradient.reshape(token_rows, KEY_VALUE_HEADS, HEAD_SIZE), cosine_table, sine_table
    )
    head_term = jnp.stack(
        [
            jnp.sum(d_query_normed * query_unit, axis=(0, 1)),
            jnp.sum(normed_key_gradient * key_unit, axis=(0, 1)),
        ]
    )
    d_query_raw = norm_back(d_query_normed, query_unit, query_root, head_gain_wide[0])
    d_key_raw = norm_back(normed_key_gradient, key_unit, key_root, head_gain_wide[1])
    d_proj_low = jnp.concatenate(
        [
            d_query_raw.reshape(token_rows, query_total_width),
            d_gate_logits,
            d_key_raw.reshape(token_rows, key_total_width),
            d_values,
        ],
        axis=1,
    ).astype(jnp.bfloat16)
    columns = lax.dot_general(
        d_proj_low,
        lax.all_gather(projection_weight, ("seq", "ctx"), axis=0, tiled=True),
        contract_cols,
        preferred_element_type=jnp.float32,
    )
    normed_rows = normed_attn
    grad_rows = d_attn_low
    attn_grads = lax.psum_scatter(
        jnp.concatenate(
            [
                lax.dot_general(
                    normed_rows, d_proj_low, contract_rows, preferred_element_type=jnp.float32
                ),
                lax.dot_general(
                    grad_rows, mixed_heads, contract_rows, preferred_element_type=jnp.float32
                ),
            ],
            axis=1,
        ).astype(jnp.bfloat16),
        ("seq", "ctx"),
        scatter_dimension=0,
        tiled=True,
    ).astype(jnp.float32)
    gain_attn_term = jnp.sum(columns * unit_attn, axis=0)
    tokens_grad = (d_resid_mid + norm_back(columns, unit_attn, root_attn, gain_attn_full)).astype(
        jnp.bfloat16
    )
    sum_attn_gain, sum_mlp_gain, sum_head_gain = lax.psum(
        (gain_attn_term, gain_mlp_term, head_term), ("rep", "seq", "ctx")
    )
    mlp_grads, attn_grads = over_replicas((mlp_grads, attn_grads))
    group_rank = lax.axis_index(("seq", "ctx"))
    attention_gain_grad = lax.dynamic_slice_in_dim(
        sum_attn_gain, group_rank * shard_rows, shard_rows, 0
    )
    feedforward_gain_grad = lax.dynamic_slice_in_dim(
        sum_mlp_gain, group_rank * shard_rows, shard_rows, 0
    )
    return (
        layer_out,
        tokens_grad,
        attention_gain_grad,
        attn_grads[:, :proj_width],
        sum_head_gain,
        attn_grads[:, proj_width:],
        feedforward_gain_grad,
        mlp_grads[:, :ff_width],
        mlp_grads[:, ff_width : 2 * ff_width],
        mlp_grads[:, 2 * ff_width :],
    )


def solution(mesh):
    in_specs = (
        P(("rep", "seq", "ctx"), None),
        P(("rep", "seq", "ctx"), None),
        P(("rep", "seq")),
        P(("rep", "seq")),
        P(("seq", "ctx")),
        P(("seq", "ctx"), None),
        P(),
        P(("seq", "ctx"), None),
        P(("seq", "ctx")),
        P(("seq", "ctx"), None),
        P(("seq", "ctx"), None),
        P(("seq", "ctx"), None),
    )
    out_specs = (
        P(("rep", "seq", "ctx"), None),
        P(("rep", "seq", "ctx"), None),
        P(("seq", "ctx")),
        P(("seq", "ctx"), None),
        P(),
        P(("seq", "ctx"), None),
        P(("seq", "ctx")),
        P(("seq", "ctx"), None),
        P(("seq", "ctx"), None),
        P(("seq", "ctx"), None),
    )
    return jax.shard_map(
        per_device, mesh=mesh, in_specs=in_specs, out_specs=out_specs, check_vma=False
    )
```

profile of v0, /device:TPU:0, one launch (start us, length us, event | category | flops | bytes accessed | tf_op | source)
XLA Modules:
  0.0 4382.5 jit_solution(18146430784652032975)
XLA Ops:
  8.0 22.4 all-gather
  30.7 462.0 %all-gather.10.cloned.1.call-done = bf16[2048,6144]{1,0:T(8,128)(2,1)} async-done(((bf16[256,6144]{1,0:T(8,128)(2,1)}), bf16[2048,6144]{1,0:T(8,128)(2,1)}) %all-gather.10.cloned.1.call-update) | async-done | bytes 25165840 | tf_op jit(solution)/shard_map/all_gather | solution.py:98
  492.8 11.7 fusion.46
  516.4 20.9 all-gather.1
  545.0 10.4 all-gather.12.cloned.1.call-done
  557.7 45.0 %all-gather.14.cloned.1.call-done = bf16[1024,1024]{0,1:T(8,128)(2,1)} async-done(((bf16[256,1024]{0,1:T(8,128)(2,1)}), bf16[1024,1024]{0,1:T(8,128)(2,1)}) %all-gather.14.cloned.1.call-update) | async-done | bytes 2097168 | tf_op jit(solution)/shard_map/all_gather | solution.py:134
  602.7 12.2 fusion.56
  615.0 8.1 fusion.3
  623.1 7.6 divide_convert_fusion
  630.7 3.2 fusion.27
  636.6 3.9 multiply_convert_fusion.6
  640.5 87.4 %all-gather.16.cloned.1.call-done = bf16[2048,2048]{1,0:T(8,128)(2,1)} async-done(((bf16[256,2048]{1,0:T(8,128)(2,1)}), bf16[2048,2048]{1,0:T(8,128)(2,1)}) %all-gather.16.cloned.1.call-update) | async-done | bytes 8388624 | tf_op jit(solution)/shard_map/all_gather | solution.py:166
  727.9 6.2 multiply_reduce_fusion.3
  734.4 473.5 %all-gather.18.cloned.1.call-done = bf16[2048,6144]{1,0:T(8,128)(2,1)} async-done(((bf16[256,6144]{1,0:T(8,128)(2,1)}), bf16[2048,6144]{1,0:T(8,128)(2,1)}) %all-gather.18.cloned.1.call-update) | async-done | bytes 25165840 | tf_op jit(solution)/shard_map/all_gather | solution.py:176
  1207.9 14.3 fusion.57
  1222.2 468.7 %all-gather.20.cloned.1.call-done = bf16[2048,6144]{1,0:T(8,128)(2,1)} async-done(((bf16[256,6144]{1,0:T(8,128)(2,1)}), bf16[2048,6144]{1,0:T(8,128)(2,1)}) %all-gather.20.cloned.1.call-update) | async-done | bytes 25165840 | tf_op jit(solution)/shard_map/all_gather | solution.py:177
  1690.9 14.3 fusion.58
  1705.3 468.9 %all-gather.22.cloned.1.call-done = bf16[2048,6144]{1,0:T(8,128)(2,1)} async-done(((bf16[256,6144]{1,0:T(8,128)(2,1)}), bf16[2048,6144]{1,0:T(8,128)(2,1)}) %all-gather.22.cloned.1.call-update) | async-done | bytes 25165840 | tf_op jit(solution)/shard_map/all_gather | solution.py:196
  2174.1 19.1 multiply_convert_fusion
  2193.2 13.5 fusion.59
  2206.7 15.2 multiply_reduce_fusion
  2224.4 8.6 multiply_convert_fusion.3
  2234.1 14.6 fusion
  2251.1 10.1 fusion.2
  2261.3 7.7 fusion.5
  2270.3 7.5 bitcast_convert_fusion
  2277.8 4.1 copy.117
  2282.0 4.7 convolution_multiply_fusion
  2298.6 4.8 fusion.22
  2303.4 5.7 convolution_convert_fusion.4
  2309.1 5.0 reduce-scatter.5.cloned.1.call-done
  2325.4 34.5 reduce-scatter.7.cloned.1.call-done
  2359.9 12.6 convolution_convert_fusion.3
  2372.5 22.9 pad_maximum_fusion.1
  2396.6 13.9 convolution_convert_fusion.1
  2410.5 14.0 convolution_convert_fusion.2
  2424.5 14.2 convolution_convert_fusion
  2438.7 50.8 %pad_maximum_fusion = bf16[2048,18432]{1,0:T(8,128)(2,1)} fusion(bf16[2048,6144]{1,0:T(8,128)(2,1)} %convolution_convert_fusion, bf16[2048,6144]{1,0:T(8,128)(2,1)} %convolution_convert_fusion.1, bf16[2048,6144]{1,0:T(8,128)(2,1)} %convolution_convert_fusion.2), kind=kLoop, calls=%fused_computation | loop fusion | flops 226492416 | bytes 150994944 | tf_op jit(solution)/shard_map/concatenate | solution.py:223
  2489.5 448.2 %reduce-scatter.9.cloned.1.call-done = bf16[256,8192]{1,0:T(8,128)(2,1)} async-done(((bf16[2048,8192]{1,0:T(8,128)(2,1)}), bf16[256,8192]{1,0:T(8,128)(2,1)}) %reduce-scatter.9.cloned.1.call-update) | async-done | bytes 4194320 | tf_op jit(solution)/shard_map/reduce_scatter | solution.py:318
  2937.7 1180.7 %reduce-scatter.11.cloned.1.call-done = bf16[256,18432]{1,0:T(8,128)(2,1)} async-done(((bf16[2048,18432]{1,0:T(8,128)(2,1)}), bf16[256,18432]{1,0:T(8,128)(2,1)}) %reduce-scatter.11.cloned.1.call-update) | async-done | bytes 9437200 | tf_op jit(solution)/shard_map/reduce_scatter | solution.py:222
  4120.0 15.0 fusion.10
  4135.1 14.9 fusion.17
  4150.0 40.8 all-reduce
  4192.0 3.2 fusion.16
  4195.1 164.5 %all-reduce.4.cloned.1.call-done = (bf16[256,8192]{1,0:T(8,128)(2,1)}, bf16[256,18432]{1,0:T(8,128)(2,1)}) async-done(((bf16[256,8192]{1,0:T(8,128)(2,1)}, bf16[256,18432]{1,0:T(8,128)(2,1)}), (bf16[256,8192]{1,0:T(8,128)(2,1)}, bf16[256,18432]{1,0:T(8,128)(2,1)})) %all-reduce.4.cloned.1.call-update) | async-done | bytes 13631504 | tf_op jit(solution)/shard_map/psum | solution.py:67
  4359.7 5.9 slice.91
  4365.6 2.8 slice.92
  4368.4 6.9 fusion.53
  (213 shorter events, 59.9 us)
Async XLA Ops:
  7.2 23.2 copy-start.16
  7.2 485.6 %all-gather.10.cloned.1.call-start = ((), (), s32[]{:S(2)}) async-start(), calls=%async_computation.4 | async-start | bytes 28311552 | tf_op jit(solution)/shard_map/all_gather | solution.py:98
  7.9 547.5 %all-gather.12.cloned.1.call-start = ((), (), s32[]{:S(2)}) async-start(), calls=%async_computation.5 | async-start | bytes 2621440 | tf_op jit(solution)/shard_map/all_gather | solution.py:135
  30.4 474.1 %copy-start.36 = (f32[8,1,256]{2,1,0:T(1,128)}, f32[8,1,256]{2,1,0:T(1,128)S(1)}, u32[]{:S(2)}) copy-start(f32[8,1,256]{2,1,0:T(1,128)S(1)} %convert_element_type.136) | copy-start | bytes 24580
  30.7 473.8 %copy-start.38 = (f32[256]{0:T(256)}, f32[256]{0:T(256)S(1)}, u32[]{:S(2)}) copy-start(f32[256]{0:T(256)S(1)} %add_rsqrt_fusion.3) | copy-start | bytes 3076
  492.8 15.4 copy-start.55
  508.1 94.6 %all-gather.14.cloned.1.call-start = ((), (), s32[]{:S(2)}) async-start(), calls=%async_computation.6 | async-start | bytes 2621440 | tf_op jit(solution)/shard_map/all_gather | solution.py:134
  508.2 32.9 copy-start.49
  508.8 33.9 copy-start.27
  508.8 33.9 copy-start.29
  513.8 214.1 %all-gather.16.cloned.1.call-start = ((), (), s32[]{:S(2)}) async-start(), calls=%async_computation.7 | async-start | bytes 9437184 | tf_op jit(solution)/shard_map/all_gather | solution.py:166
  514.4 693.5 %all-gather.18.cloned.1.call-start = ((), (), s32[]{:S(2)}) async-start(), calls=%async_computation.8 | async-start | bytes 28311552 | tf_op jit(solution)/shard_map/all_gather | solution.py:176
  515.0 22.3 copy-start.52
  515.0 22.4 copy-start.53
  515.0 1175.9 %all-gather.20.cloned.1.call-start = ((), (), s32[]{:S(2)}) async-start(), calls=%async_computation.9 | async-start | bytes 28311552 | tf_op jit(solution)/shard_map/all_gather | solution.py:177
  515.6 1658.5 %all-gather.22.cloned.1.call-start = ((), (), s32[]{:S(2)}) async-start(), calls=%async_computation.10 | async-start | bytes 28311552 | tf_op jit(solution)/shard_map/all_gather | solution.py:196
  516.3 1797.7 %reduce-scatter.5.cloned.1.call-start = ((), (), s32[]{:S(2)}) async-start(), calls=%async_computation.11 | async-start | bytes 2621440 | tf_op jit(solution)/shard_map/reduce_scatter | solution.py:274
  543.7 59.0 %copy-start.14 = (bf16[256,16,64]{2,0,1:T(8,128)(2,1)}, bf16[256,16,64]{2,0,1:T(8,128)(2,1)S(1)}, u32[]{:S(2)}) copy-start(bf16[256,16,64]{2,0,1:T(8,128)(2,1)S(1)} %copy.80) | copy-start | bytes 1572868
  557.7 73.0 %copy-start.7 = (bf16[128,8,8,128]{3,2,1,0:T(8,128)(2,1)}, bf16[128,8,8,128]{3,2,1,0:T(8,128)(2,1)S(1)}, u32[]{:S(2)}) copy-start(bf16[128,8,8,128]{3,2,1,0:T(8,128)(2,1)S(1)} %copy.123) | copy-start | bytes 6291460
  615.0 8.1 copy-start.40
  636.6 91.3 %copy-start.17 = (bf16[256,2048]{1,0:T(8,128)(2,1)S(1)}, bf16[256,2048]{1,0:T(8,128)(2,1)}, u32[]{:S(2)}) copy-start(bf16[256,2048]{1,0:T(8,128)(2,1)} %param.12) | copy-start | bytes 3145732
  734.1 1487.8 %copy-start.19 = (f32[256,2048]{1,0:T(8,128)}, f32[256,2048]{1,0:T(8,128)S(1)}, u32[]{:S(2)}) copy-start(f32[256,2048]{1,0:T(8,128)S(1)} %get-tuple-element.54) | copy-start | bytes 6291460
  734.4 956.6 %copy-start.11 = (bf16[256,2048]{1,0:T(8,128)(2,1)}, bf16[256,2048]{1,0:T(8,128)(2,1)S(1)}, u32[]{:S(2)}) copy-start(bf16[256,2048]{1,0:T(8,128)(2,1)S(1)} %multiply_convert_fusion.5) | copy-start | bytes 3145732
  2206.7 15.2 copy-start.23
  2224.3 8.6 copy-start.4
  2224.3 9.1 copy-start.41
  2224.3 9.1 copy-start.43
  2234.1 14.7 slice-start
  2234.1 14.7 slice-start.1
  2234.1 15.9 slice-start.2
  2234.1 17.1 slice-start.3
  2251.1 10.1 copy-start.15
  2261.3 7.8 copy-start.48
  2261.3 8.4 copy-start.50
  2269.0 90.8 %reduce-scatter.7.cloned.1.call-start = ((), (), s32[]{:S(2)}) async-start(), calls=%async_computation.12 | async-start | bytes 2621440 | tf_op jit(solution)/shard_map/reduce_scatter | solution.py:280
  2281.9 655.8 %reduce-scatter.9.cloned.1.call-start = ((), (), s32[]{:S(2)}) async-start(), calls=%async_computation.13 | async-start | bytes 37748736 | tf_op jit(solution)/shard_map/reduce_scatter | solution.py:318
  2303.4 56.5 %copy-start.25 = (bf16[256,2048]{1,0:T(8,128)(2,1)}, bf16[256,2048]{1,0:T(8,128)(2,1)S(1)}, u32[]{:S(2)}) copy-start(bf16[256,2048]{1,0:T(8,128)(2,1)S(1)} %get-tuple-element.27) | copy-start | bytes 3145732
  2322.3 37.6 copy-start.18
  2322.3 37.6 copy-start.37
  2322.3 37.6 copy-start.39
  2325.3 47.1 %copy-start.31 = (bf16[256,1024]{1,0:T(8,128)(2,1)}, bf16[256,1024]{1,0:T(8,128)(2,1)S(1)}, u32[]{:S(2)}) copy-start(bf16[256,1024]{1,0:T(8,128)(2,1)S(1)} %get-tuple-element.32) | copy-start | bytes 1572868
  2395.4 1723.1 %reduce-scatter.11.cloned.1.call-start = ((), (), s32[]{:S(2)}) async-start(), calls=%async_computation.14 | async-start | bytes 84934656 | tf_op jit(solution)/shard_map/reduce_scatter | solution.py:222
  2410.5 14.0 copy-start.24
  2489.5 1870.2 %all-reduce.4.cloned.1.call-start = ((), (), s32[]{:S(2)}) async-start(), calls=%async_computation.15 | async-start | bytes 27262976 | tf_op jit(solution)/shard_map/psum | solution.py:67
  4120.0 15.0 copy-start.45
  4135.1 14.9 copy-start.51
  4135.1 56.9 %copy-start.6 = (f32[256,2048]{1,0:T(8,128)S(1)}, f32[256,2048]{1,0:T(8,128)}, u32[]{:S(2)}) copy-start(f32[256,2048]{1,0:T(8,128)} %copy-done.4) | copy-start | bytes 6291460
  4359.7 8.7 copy-start.1
  (25 other events, 75.0 us)
Sparse Core Ops, SparseCore 0:
  9.6 483.1 all-gather.9
  508.2 47.1 all-gather.11
  557.6 45.0 all-gather.13
  604.7 123.1 all-gather.15
  729.3 478.5 all-gather.17
  1209.3 481.6 all-gather.19
  1692.5 481.6 all-gather.21
  2269.1 44.8 reduce-scatter.4
  2316.5 43.3 reduce-scatter.6
  2395.5 542.1 reduce-scatter.8
  2941.6 1176.8 reduce-scatter.10
  4121.1 238.5 all-reduce.3
where the time goes:
time: 4390 us; the launch traced here: 4380 us
  waiting for transfers between devices  3850 us (88%)
  matrix products  243 us (6%)
  other arithmetic  130 us (3%)
  blocking collectives  84 us (2%)
  local copies, waits for them, and re-layouts  57.2 us (1%)
    reduce_scatter x1, waiting for transfers between devices, per_device(): lax.psum_scatter(jnp.concatenate([lax.dot_general(normed_rows, d_gate_low...  1180 us
    all_gather x1, waiting for transfers between devices, per_device(): gate_piece = lax.all_gather(gate_weight, ('seq', 'ctx'), axis=0, tiled=True)  474 us
    all_gather x1, waiting for transfers between devices, per_device(): lax.all_gather(down_weight, ('seq', 'ctx'), axis=0, tiled=True)  469 us
    all_gather x1, waiting for transfers between devices, per_device(): up_piece = lax.all_gather(up_weight, ('seq', 'ctx'), axis=0, tiled=True)  469 us
    all_gather x1, waiting for transfers between devices, per_device(): lax.all_gather(projection_weight, ('seq', 'ctx'), axis=0, tiled=True)  462 us
    reduce_scatter x1, waiting for transfers between devices, per_device(): lax.psum_scatter(jnp.concatenate([lax.dot_general(normed_rows, d_proj_low...  448 us
    psum x1, waiting for transfers between devices, over_replicas(): lax.psum(grad_parts[1].astype(jnp.bfloat16), 'rep').astype(jnp.float32)  165 us
  transfers between devices with their start and end apart: 12, of which 12 were waited for; matrix products, arithmetic and copies ran while one was open for 6% of the time, Pallas kernels for 0%

commit v1 on v0

--- a/solution.py
+++ b/solution.py
@@ -173,8 +173,13 @@
     root_mlp = lax.rsqrt(jnp.mean(resid_mid * resid_mid, axis=1, keepdims=True) + norm_epsilon)
     unit_mlp = resid_mid * root_mlp
     gain_piece = lax.all_gather(feedforward_gain, ("seq", "ctx"), axis=0, tiled=True)
-    gate_piece = lax.all_gather(gate_weight, ("seq", "ctx"), axis=0, tiled=True)
-    up_piece = lax.all_gather(up_weight, ("seq", "ctx"), axis=0, tiled=True)
+    gate_piece, up_piece = jnp.split(
+        lax.all_gather(
+            jnp.concatenate([gate_weight, up_weight], axis=1), ("seq", "ctx"), axis=0, tiled=True
+        ),
+        [gate_weight.shape[1]],
+        axis=1,
+    )
     columns = unit_mlp
     normed = (columns * gain_piece.astype(jnp.float32)).astype(jnp.bfloat16)
     result = (

time: 4390 us -> 5310 us (1.21)
  waiting for transfers between devices: 3850 us -> 4770 us
    all_gather x0 -> x1, waiting for transfers between devices: none -> 945 us  [per_device(): lax.all_gather(jnp.concatenate([gate_weight, up_weight], axis=1), ('seq',...]
  transfers between devices with their start and end apart: 12 -> 13, of which waited for: 12 -> 13; matrix products, arithmetic and copies ran while one was open for 6% -> 6% of each run, Pallas kernels for 0% -> 0%
where the time goes in v1:
time: 5310 us; the launch traced here: 5300 us
  waiting for transfers between devices  4770 us (90%)
  matrix products  242 us (5%)
  other arithmetic  137 us (3%)
  blocking collectives  84.4 us (2%)
  local copies, waits for them, and re-layouts  58.2 us (1%)
    reduce_scatter x1, waiting for transfers between devices, per_device(): lax.psum_scatter(jnp.concatenate([lax.dot_general(normed_rows, d_gate_low...  1180 us
    all_gather x1, waiting for transfers between devices, per_device(): lax.all_gather(jnp.concatenate([gate_weight, up_weight], axis=1), ('seq',...  945 us
    all_gather x1, waiting for transfers between devices, per_device(): up_piece = lax.all_gather(up_weight, ('seq', 'ctx'), axis=0, tiled=True)  470 us
    all_gather x1, waiting for transfers between devices, per_device(): gate_piece = lax.all_gather(gate_weight, ('seq', 'ctx'), axis=0, tiled=True)  463 us
    all_gather x1, waiting for transfers between devices, per_device(): lax.all_gather(projection_weight, ('seq', 'ctx'), axis=0, tiled=True)  462 us
    all_gather x1, waiting for transfers between devices, per_device(): lax.all_gather(down_weight, ('seq', 'ctx'), axis=0, tiled=True)  457 us
    reduce_scatter x1, waiting for transfers between devices, per_device(): lax.psum_scatter(jnp.concatenate([lax.dot_general(normed_rows, d_proj_low...  449 us
    psum x1, waiting for transfers between devices, over_replicas(): lax.psum(grad_parts[1].astype(jnp.bfloat16), 'rep').astype(jnp.float32)  165 us
  transfers between devices with their start and end apart: 13, of which 13 were waited for; matrix products, arithmetic and copies ran while one was open for 6% of the time, Pallas kernels for 0%

profile of v1, /device:TPU:0, one launch (start us, length us, event | category | flops | bytes accessed | tf_op | source)
XLA Modules:
  0.0 5304.8 jit_solution(2832167608420305301)
XLA Ops:
  8.0 22.4 all-gather
  30.7 462.0 %all-gather.11.cloned.1.call-done = bf16[2048,6144]{1,0:T(8,128)(2,1)} async-done(((bf16[256,6144]{1,0:T(8,128)(2,1)}), bf16[2048,6144]{1,0:T(8,128)(2,1)}) %all-gather.11.cloned.1.call-update) | async-done | bytes 25165840 | tf_op jit(solution)/shard_map/all_gather | solution.py:98
  492.8 11.7 fusion.50
  516.2 5.3 pad_maximum_fusion.2
  523.7 21.2 all-gather.1
  557.7 44.9 all-gather.15.cloned.1.call-done
  602.7 12.2 fusion.60
  614.9 8.0 fusion.7
  622.9 7.6 divide_convert_fusion
  630.6 3.2 fusion.31
  636.5 3.9 multiply_convert_fusion.6
  640.4 87.5 %all-gather.17.cloned.1.call-done = bf16[2048,2048]{1,0:T(8,128)(2,1)} async-done(((bf16[256,2048]{1,0:T(8,128)(2,1)}), bf16[2048,2048]{1,0:T(8,128)(2,1)}) %all-gather.17.cloned.1.call-update) | async-done | bytes 8388624 | tf_op jit(solution)/shard_map/all_gather | solution.py:166
  727.9 6.2 multiply_reduce_fusion.3
  735.0 945.3 %all-gather.19.cloned.1.call-done = bf16[2048,12288]{1,0:T(8,128)(2,1)} async-done(((bf16[256,12288]{1,0:T(8,128)(2,1)}), bf16[2048,12288]{1,0:T(8,128)(2,1)}) %all-gather.19.cloned.1.call-update) | async-done | bytes 50331664 | tf_op jit(solution)/shard_map/all_gather | solution.py:177
  1680.3 13.3 fusion.2
  1693.6 13.2 fusion
  1706.8 456.5 %all-gather.21.cloned.1.call-done = bf16[2048,6144]{1,0:T(8,128)(2,1)} async-done(((bf16[256,6144]{1,0:T(8,128)(2,1)}), bf16[2048,6144]{1,0:T(8,128)(2,1)}) %all-gather.21.cloned.1.call-update) | async-done | bytes 25165840 | tf_op jit(solution)/shard_map/all_gather | solution.py:201
  2163.4 20.1 multiply_convert_fusion
  2183.5 463.0 %all-gather.23.cloned.1.call-done = bf16[2048,6144]{1,0:T(8,128)(2,1)} async-done(((bf16[256,6144]{1,0:T(8,128)(2,1)}), bf16[2048,6144]{1,0:T(8,128)(2,1)}) %all-gather.23.cloned.1.call-update) | async-done | bytes 25165840 | tf_op jit(solution)/shard_map/all_gather | solution.py:219
  2646.5 13.6 fusion.61
  2660.1 469.6 %all-gather.25.cloned.1.call-done = bf16[2048,6144]{1,0:T(8,128)(2,1)} async-done(((bf16[256,6144]{1,0:T(8,128)(2,1)}), bf16[2048,6144]{1,0:T(8,128)(2,1)}) %all-gather.25.cloned.1.call-update) | async-done | bytes 25165840 | tf_op jit(solution)/shard_map/all_gather | solution.py:220
  3129.7 15.2 multiply_reduce_fusion
  3147.4 8.5 multiply_convert_fusion.3
  3156.5 14.6 fusion.4
  3173.5 10.2 fusion.6
  3183.7 7.7 fusion.9
  3192.7 7.5 bitcast_convert_fusion
  3200.3 4.1 copy.117
  3204.4 4.7 convolution_multiply_fusion
  3221.0 4.8 fusion.26
  3225.8 5.7 convolution_convert_fusion.4
  3231.5 5.2 reduce-scatter.5.cloned.1.call-done
  3248.0 34.2 reduce-scatter.7.cloned.1.call-done
  3282.2 12.6 convolution_convert_fusion.3
  3294.8 22.6 pad_maximum_fusion.1
  3318.7 13.9 convolution_convert_fusion.1
  3332.6 14.0 convolution_convert_fusion.2
  3346.6 14.2 convolution_convert_fusion
  3360.8 50.7 pad_maximum_fusion
  3411.6 448.8 %reduce-scatter.9.cloned.1.call-done = bf16[256,8192]{1,0:T(8,128)(2,1)} async-done(((bf16[2048,8192]{1,0:T(8,128)(2,1)}), bf16[256,8192]{1,0:T(8,128)(2,1)}) %reduce-scatter.9.cloned.1.call-update) | async-done | bytes 4194320 | tf_op jit(solution)/shard_map/reduce_scatter | solution.py:323
  3860.4 1180.6 %reduce-scatter.11.cloned.1.call-done = bf16[256,18432]{1,0:T(8,128)(2,1)} async-done(((bf16[2048,18432]{1,0:T(8,128)(2,1)}), bf16[256,18432]{1,0:T(8,128)(2,1)}) %reduce-scatter.11.cloned.1.call-update) | async-done | bytes 9437200 | tf_op jit(solution)/shard_map/reduce_scatter | solution.py:227
  5042.5 15.0 fusion.14
  5057.6 14.9 fusion.21
  5072.4 40.8 all-reduce
  5114.5 3.2 fusion.20
  5117.7 164.6 %all-reduce.4.cloned.1.call-done = (bf16[256,8192]{1,0:T(8,128)(2,1)}, bf16[256,18432]{1,0:T(8,128)(2,1)}) async-done(((bf16[256,8192]{1,0:T(8,128)(2,1)}, bf16[256,18432]{1,0:T(8,128)(2,1)}), (bf16[256,8192]{1,0:T(8,128)(2,1)}, bf16[256,18432]{1,0:T(8,128)(2,1)})) %all-reduce.4.cloned.1.call-update) | async-done | bytes 13631504 | tf_op jit(solution)/shard_map/psum | solution.py:67
  5282.3 5.9 slice.91
  5291.0 6.9 fusion.57
  (213 shorter events, 67.6 us)
Async XLA Ops:
  7.2 23.2 copy-start.17
  7.2 485.6 %all-gather.11.cloned.1.call-start = ((), (), s32[]{:S(2)}) async-start(), calls=%async_computation.4 | async-start | bytes 28311552 | tf_op jit(solution)/shard_map/all_gather | solution.py:98
  7.9 547.6 %all-gather.13.cloned.1.call-start = ((), (), s32[]{:S(2)}) async-start(), calls=%async_computation.5 | async-start | bytes 2621440 | tf_op jit(solution)/shard_map/all_gather | solution.py:135
  30.4 474.1 %copy-start.38 = (f32[8,1,256]{2,1,0:T(1,128)}, f32[8,1,256]{2,1,0:T(1,128)S(1)}, u32[]{:S(2)}) copy-start(f32[8,1,256]{2,1,0:T(1,128)S(1)} %convert_element_type.136) | copy-start | bytes 24580
  30.7 473.8 %copy-start.40 = (f32[256]{0:T(256)}, f32[256]{0:T(256)S(1)}, u32[]{:S(2)}) copy-start(f32[256]{0:T(256)S(1)} %add_rsqrt_fusion.3) | copy-start | bytes 3076
  492.8 15.4 copy-start.53
  508.1 94.6 %all-gather.15.cloned.1.call-start = ((), (), s32[]{:S(2)}) async-start(), calls=%async_computation.6 | async-start | bytes 2621440 | tf_op jit(solution)/shard_map/all_gather | solution.py:134
  508.2 41.0 copy-start.47
  508.8 42.1 copy-start.28
  508.8 42.1 copy-start.30
  515.6 212.3 %all-gather.17.cloned.1.call-start = ((), (), s32[]{:S(2)}) async-start(), calls=%async_computation.7 | async-start | bytes 9437184 | tf_op jit(solution)/shard_map/all_gather | solution.py:166
  516.1 1164.2 %all-gather.19.cloned.1.call-start = ((), (), s32[]{:S(2)}) async-start(), calls=%async_computation.8 | async-start | bytes 56623104 | tf_op jit(solution)/shard_map/all_gather | solution.py:177
  521.5 1641.9 %all-gather.21.cloned.1.call-start = ((), (), s32[]{:S(2)}) async-start(), calls=%async_computation.9 | async-start | bytes 28311552 | tf_op jit(solution)/shard_map/all_gather | solution.py:201
  522.1 22.8 copy-start.50
  522.1 22.9 copy-start.51
  522.1 2124.4 %all-gather.23.cloned.1.call-start = ((), (), s32[]{:S(2)}) async-start(), calls=%async_computation.10 | async-start | bytes 28311552 | tf_op jit(solution)/shard_map/all_gather | solution.py:219
  522.9 2606.9 %all-gather.25.cloned.1.call-start = ((), (), s32[]{:S(2)}) async-start(), calls=%async_computation.11 | async-start | bytes 28311552 | tf_op jit(solution)/shard_map/all_gather | solution.py:220
  523.6 2713.1 %reduce-scatter.5.cloned.1.call-start = ((), (), s32[]{:S(2)}) async-start(), calls=%async_computation.12 | async-start | bytes 2621440 | tf_op jit(solution)/shard_map/reduce_scatter | solution.py:279
  552.0 50.7 copy-start.15
  552.0 50.7 copy-start.32
  557.7 72.9 %copy-start.7 = (bf16[128,8,8,128]{3,2,1,0:T(8,128)(2,1)}, bf16[128,8,8,128]{3,2,1,0:T(8,128)(2,1)S(1)}, u32[]{:S(2)}) copy-start(bf16[128,8,8,128]{3,2,1,0:T(8,128)(2,1)S(1)} %copy.123) | copy-start | bytes 6291460
  636.5 91.4 %copy-start.18 = (bf16[256,2048]{1,0:T(8,128)(2,1)S(1)}, bf16[256,2048]{1,0:T(8,128)(2,1)}, u32[]{:S(2)}) copy-start(bf16[256,2048]{1,0:T(8,128)(2,1)} %param.12) | copy-start | bytes 3145732
  734.1 2410.9 %copy-start.20 = (f32[256,2048]{1,0:T(8,128)}, f32[256,2048]{1,0:T(8,128)S(1)}, u32[]{:S(2)}) copy-start(f32[256,2048]{1,0:T(8,128)S(1)} %get-tuple-element.54) | copy-start | bytes 6291460
  735.0 958.6 %copy-start.11 = (bf16[256,2048]{1,0:T(8,128)(2,1)}, bf16[256,2048]{1,0:T(8,128)(2,1)S(1)}, u32[]{:S(2)}) copy-start(bf16[256,2048]{1,0:T(8,128)(2,1)S(1)} %multiply_convert_fusion.5) | copy-start | bytes 3145732
  3129.7 15.2 copy-start.24
  3147.4 8.5 copy-start.4
  3156.4 14.7 slice-start
  3156.4 14.7 slice-start.1
  3156.5 15.9 slice-start.2
  3156.5 17.0 slice-start.3
  3173.5 10.2 copy-start.16
  3183.7 7.8 copy-start.46
  3183.7 8.4 copy-start.48
  3191.5 90.7 %reduce-scatter.7.cloned.1.call-start = ((), (), s32[]{:S(2)}) async-start(), calls=%async_computation.13 | async-start | bytes 2621440 | tf_op jit(solution)/shard_map/reduce_scatter | solution.py:285
  3204.4 656.0 %reduce-scatter.9.cloned.1.call-start = ((), (), s32[]{:S(2)}) async-start(), calls=%async_computation.14 | async-start | bytes 37748736 | tf_op jit(solution)/shard_map/reduce_scatter | solution.py:323
  3210.3 5.1 copy-start.31
  3225.8 56.4 %copy-start.26 = (bf16[256,2048]{1,0:T(8,128)(2,1)}, bf16[256,2048]{1,0:T(8,128)(2,1)S(1)}, u32[]{:S(2)}) copy-start(bf16[256,2048]{1,0:T(8,128)(2,1)S(1)} %get-tuple-element.27) | copy-start | bytes 3145732
  3244.9 37.3 copy-start.19
  3245.0 37.3 copy-start.39
  3245.0 37.3 copy-start.41
  3248.0 46.8 copy-start.33
  3317.5 1723.4 %reduce-scatter.11.cloned.1.call-start = ((), (), s32[]{:S(2)}) async-start(), calls=%async_computation.15 | async-start | bytes 84934656 | tf_op jit(solution)/shard_map/reduce_scatter | solution.py:227
  3332.6 14.0 copy-start.25
  3411.5 1870.8 %all-reduce.4.cloned.1.call-start = ((), (), s32[]{:S(2)}) async-start(), calls=%async_computation.16 | async-start | bytes 27262976 | tf_op jit(solution)/shard_map/psum | solution.py:67
  5042.5 15.0 copy-start.43
  5057.5 14.9 copy-start.49
  5057.5 57.0 %copy-start.6 = (f32[256,2048]{1,0:T(8,128)S(1)}, f32[256,2048]{1,0:T(8,128)}, u32[]{:S(2)}) copy-start(f32[256,2048]{1,0:T(8,128)} %copy-done.4) | copy-start | bytes 6291460
  5282.3 8.7 copy-start.1
  (24 other events, 65.1 us)
Sparse Core Ops, SparseCore 0:
  9.6 483.1 all-gather.10
  508.2 47.2 all-gather.12
  557.7 44.9 all-gather.14
  604.6 123.1 all-gather.16
  729.8 950.4 all-gather.18
  1681.7 481.6 all-gather.20
  2164.9 481.6 all-gather.22
  2648.1 481.6 all-gather.24
  3191.6 45.0 reduce-scatter.4
  3239.0 43.2 reduce-scatter.6
  3317.6 542.6 reduce-scatter.8
  3864.1 1176.8 reduce-scatter.10
  5043.7 238.5 all-reduce.3
